TPU v7x, 768 devices: a whole 4x8x12 slice. The times are simulated.
768 devices in a mesh: section: 16 (over x, y_hi), tp: 48 (over y_lo, z, core).
Axes of the slice: x: 4, y: 8 (y_hi: 4, y_lo: 2; y = y_hi * 2 + y_lo), z: 12, core: 2. Of those that a mesh axis runs over, the one named last changes fastest.
Arguments:
- queries_now: bfloat16 [16, 6144, 4096], P('section', 'tp'), may hold values from -6 to 6
- stash_now: bfloat16 [16, 6144, 1024], P('section', 'tp'), may hold values from -6 to 6
- positions_now: int32 [16, 6144], P('section', 'tp'), may hold values from 0 to 127, as said below
- queries_old: bfloat16 [16, 6144, 4096], P('section', 'tp'), may hold values from -6 to 6
- positions_old: int32 [16, 6144], P('section', 'tp'), may hold values from 0 to 127, as said below
- stash_kept: bfloat16 [16, 3072, 1024], P('section', 'tp'), may hold values from -6 to 6
- stash_held: bfloat16 [16, 3072, 1024], P('section', 'tp'), may hold values from -6 to 6
Outputs:
- mixed_now: bfloat16 [16, 6144, 4096], P('section', 'tp')
- mixed_old: bfloat16 [16, 6144, 4096], P('section', 'tp')
- stash_stored: bfloat16 [16, 3072, 1024], P('section', 'tp')
Inputs may be any that keep to these rules, and one draw needn't show every extreme that they name: `positions_now`: positions restart at 0 at the first token of each reaction and rise by one within it; a reaction has at most 128 tokens. `positions_old`: positions restart at 0 at the first token of each reaction and rise by one within it; a reaction has at most 128 tokens.
All inputs are finite; a program needn't handle non-finite values.
Results may differ from a plain program's by a relative error of at most 0.003.
Values may be sent and summed in bfloat16 or wider, within the bound.
A program may use at most 32 MiB of HBM per device.

v0:
```python
import jax
import jax.numpy as jnp
from jax import lax
from jax.sharding import PartitionSpec as P

KV_HEADS = 4
HEAD_DIM = 128
GROUP = 8


def swapped(value, axis, distance):
    mask = 2**distance
    pairs = [(source, source ^ mask) for source in range(lax.axis_size(axis))]
    return lax.ppermute(value, axis, pairs)


def shifted(value, axis, steps):
    count = lax.axis_size(axis)
    initial, last = (max(0, -steps), min(count, count - steps))
    return lax.ppermute(value, axis, [(source, source + steps) for source in range(initial, last)])


def block_attention(queries, prior, resident, positions):
    row_count = queries.shape[0]
    out_width = queries.shape[1]
    kv_width = resident.shape[1] // 2
    joined = jnp.concatenate([prior, resident], 0)
    key_rows = joined[:, :kv_width].reshape(2 * row_count, KV_HEADS, HEAD_DIM)
    value_rows = joined[:, kv_width:].reshape(2 * row_count, KV_HEADS, HEAD_DIM)
    grouped = queries.reshape(row_count, KV_HEADS, GROUP, HEAD_DIM)
    scores = jnp.einsum(
        "tkgd,skd->kgts", grouped, key_rows, preferred_element_type=jnp.float32
    ) * HEAD_DIM ** (-0.5)
    query_index = jnp.arange(row_count, dtype=jnp.int32)
    key_index = jnp.arange(2 * row_count, dtype=jnp.int32) - row_count
    visible = (key_index[None, :] <= query_index[:, None]) & (
        key_index[None, :] >= (query_index - positions)[:, None]
    )
    scores = jnp.where(visible, scores, -1e30)
    row_peak = jnp.max(scores, axis=-1, keepdims=True)
    raised = jnp.exp(scores - row_peak)
    row_total = jnp.sum(raised, axis=-1)
    weights = raised.astype(jnp.bfloat16)
    summed = jnp.einsum("kgts,skd->tkgd", weights, value_rows, preferred_element_type=jnp.float32)
    result = summed / jnp.transpose(row_total, (2, 0, 1))[..., None]
    return result.astype(jnp.bfloat16).reshape(row_count, out_width)


def body(queries_now, stash_now, positions_now, queries_old, positions_old, stash_kept, stash_held):
    tokens = stash_now.shape[1]
    evict_rows = stash_kept.shape[1]
    resident_now = stash_now[0]
    payload = jnp.stack([resident_now[tokens - evict_rows :], stash_held[0]])
    sections = lax.axis_size("section")
    for bit_number in range(sections.bit_length() - 1):
        payload = swapped(payload, "section", bit_number)
    arrived = payload[0]
    resident_old = jnp.concatenate([stash_kept[0], payload[1]], 0)
    priors = shifted(jnp.stack([resident_now, resident_old]), "tp", 1)
    prior_now = priors[0]
    prior_old = priors[1]
    mixed_now = block_attention(queries_now[0], prior_now, resident_now, positions_now[0])
    mixed_old = block_attention(queries_old[0], prior_old, resident_old, positions_old[0])
    return (mixed_now[None], mixed_old[None], arrived[None])


def solution(mesh):
    return jax.shard_map(
        body,
        mesh=mesh,
        in_specs=(
            P("section", "tp", None),
            P("section", "tp", None),
            P("section", "tp"),
            P("section", "tp", None),
            P("section", "tp"),
            P("section", "tp", None),
            P("section", "tp", None),
        ),
        out_specs=(P("section", "tp", None), P("section", "tp", None), P("section", "tp", None)),
        check_vma=False,
    )
```

profile of v0, /device:TPU:12, one launch (start us, length us, event | category | flops | bytes accessed | tf_op | source)
XLA Modules:
  0.0 126.2 jit_solution(6497062784446255074)
XLA Ops:
  0.6 0.0 copy-start.1
  0.6 1.1 copy.21
  1.8 0.1 slice.37
  1.9 1.1 copy.20
  3.0 0.0 copy-start.2
  3.0 0.1 pad_maximum_fusion
  3.1 4.5 %collective-permute-start = (bf16[2,64,1024]{1,2,0:T(8,128)(2,1)S(1)}, bf16[2,64,1024]{1,2,0:T(8,128)(2,1)S(1)}, u32[]{:S(2)}, u32[]{:S(2)}) collective-permute-start(bf16[2,64,1024]{1,2,0:T(8,128)(2,1)S(1)} %pad_maximum_fusion), channel_id=1, source_target_pairs={{0,48},{48,0},{96,144},{144,96},{192,240},{240,192},{288,336},{336... | collective-permute-start | bytes 786440 | tf_op jit(solution)/shard_map/ppermute | solution.py:14
  7.6 22.3 %collective-permute-done = bf16[2,64,1024]{1,2,0:T(8,128)(2,1)S(1)} collective-permute-done((bf16[2,64,1024]{1,2,0:T(8,128)(2,1)S(1)}, bf16[2,64,1024]{1,2,0:T(8,128)(2,1)S(1)}, u32[]{:S(2)}, u32[]{:S(2)}) %collective-permute-start) | collective-permute-done | bytes 262176 | tf_op jit(solution)/shard_map/ppermute | solution.py:14
  29.9 5.1 %collective-permute-start.1 = (bf16[2,64,1024]{1,2,0:T(8,128)(2,1)S(1)}, bf16[2,64,1024]{1,2,0:T(8,128)(2,1)S(1)}, u32[]{:S(2)}, u32[]{:S(2)}) collective-permute-start(bf16[2,64,1024]{1,2,0:T(8,128)(2,1)S(1)} %collective-permute-done), channel_id=1, source_target_pairs={{0,96},{48,144},{96,0},{144,48},{192,288},{240,336},{288,192},{336... | collective-permute-start | bytes 786440 | tf_op jit(solution)/shard_map/ppermute | solution.py:14
  35.1 14.9 %collective-permute-done.1 = bf16[2,64,1024]{1,2,0:T(8,128)(2,1)S(1)} collective-permute-done((bf16[2,64,1024]{1,2,0:T(8,128)(2,1)S(1)}, bf16[2,64,1024]{1,2,0:T(8,128)(2,1)S(1)}, u32[]{:S(2)}, u32[]{:S(2)}) %collective-permute-start.1) | collective-permute-done | bytes 262176 | tf_op jit(solution)/shard_map/ppermute | solution.py:14
  50.0 3.1 %collective-permute-start.2 = (bf16[2,64,1024]{1,2,0:T(8,128)(2,1)S(1)}, bf16[2,64,1024]{1,2,0:T(8,128)(2,1)S(1)}, u32[]{:S(2)}, u32[]{:S(2)}) collective-permute-start(bf16[2,64,1024]{1,2,0:T(8,128)(2,1)S(1)} %collective-permute-done.1), channel_id=1, source_target_pairs={{0,192},{48,240},{96,288},{144,336},{192,0},{240,48},{288,96},{336... | collective-permute-start | bytes 786440 | tf_op jit(solution)/shard_map/ppermute | solution.py:14
  53.1 11.7 %collective-permute-done.2 = bf16[2,64,1024]{1,2,0:T(8,128)(2,1)S(1)} collective-permute-done((bf16[2,64,1024]{1,2,0:T(8,128)(2,1)S(1)}, bf16[2,64,1024]{1,2,0:T(8,128)(2,1)S(1)}, u32[]{:S(2)}, u32[]{:S(2)}) %collective-permute-start.2) | collective-permute-done | bytes 262176 | tf_op jit(solution)/shard_map/ppermute | solution.py:14
  64.8 2.4 %collective-permute-start.3 = (bf16[2,64,1024]{1,2,0:T(8,128)(2,1)S(1)}, bf16[2,64,1024]{1,2,0:T(8,128)(2,1)}, u32[]{:S(2)}, u32[]{:S(2)}) collective-permute-start(bf16[2,64,1024]{1,2,0:T(8,128)(2,1)S(1)} %collective-permute-done.2), channel_id=1, source_target_pairs={{0,384},{48,432},{96,480},{144,528},{192,576},{240,624},{288,672},... | collective-permute-start | bytes 786440 | tf_op jit(solution)/shard_map/ppermute | solution.py:14
  67.2 1.1 copy.18
  68.3 1.4 %copy.42 = bf16[16,8,32,128]{3,2,1,0:T(8,128)(2,1)S(1)} copy(bf16[16,8,32,128]{3,1,2,0:T(8,128)(2,1)} %bitcast.85) | data formatting | bytes 2097152
  69.8 1.4 %copy.43 = bf16[16,8,32,128]{3,2,1,0:T(8,128)(2,1)S(1)} copy(bf16[16,8,32,128]{3,1,2,0:T(8,128)(2,1)} %bitcast.86) | data formatting | bytes 2097152
  71.2 0.0 copy-done.1
  71.2 9.1 %collective-permute-done.3 = bf16[2,64,1024]{1,2,0:T(8,128)(2,1)} collective-permute-done((bf16[2,64,1024]{1,2,0:T(8,128)(2,1)S(1)}, bf16[2,64,1024]{1,2,0:T(8,128)(2,1)}, u32[]{:S(2)}, u32[]{:S(2)}) %collective-permute-start.3) | collective-permute-done | bytes 262176 | tf_op jit(solution)/shard_map/ppermute | solution.py:14
  80.3 1.1 fusion.35
  81.4 0.1 maximum_bitcast_fusion
  81.6 0.8 pad_maximum_fusion.1
  82.4 1.9 %collective-permute-start.4 = (bf16[2,128,1024]{1,2,0:T(8,128)(2,1)}, bf16[2,128,1024]{1,2,0:T(8,128)(2,1)}, u32[]{:S(2)}, u32[]{:S(2)}) collective-permute-start(bf16[2,128,1024]{1,2,0:T(8,128)(2,1)} %pad_maximum_fusion.1), channel_id=1, source_target_pairs={{0,1},{1,2},{2,3},{3,4},{4,5},{5,6},{6,7},{7,8},{8,9},{9,10},{10,1... | collective-permute-start | bytes 1572872 | tf_op jit(solution)/shard_map/ppermute | solution.py:20
  84.3 0.0 copy-done.2
  84.4 0.1 fusion.29
  84.5 0.8 copy.31
  85.3 27.8 %collective-permute-done.4 = bf16[2,128,1024]{1,2,0:T(8,128)(2,1)} collective-permute-done((bf16[2,128,1024]{1,2,0:T(8,128)(2,1)}, bf16[2,128,1024]{1,2,0:T(8,128)(2,1)}, u32[]{:S(2)}, u32[]{:S(2)}) %collective-permute-start.4) | collective-permute-done | bytes 524320 | tf_op jit(solution)/shard_map/ppermute | solution.py:20
  113.1 1.1 slice_bitcast_fusion
  114.1 0.2 pad_maximum_fusion.2
  114.4 0.1 fusion.28
  114.4 1.1 fusion.5
  115.5 0.0 copy-start
  115.5 1.1 fusion.4
  116.6 2.3 %fusion = (f32[4,8,128]{2,1,0:T(8,128)S(1)}, f32[4,8,128]{2,1,0:T(8,128)S(1)}) fusion(f32[4,256,128,8]{2,1,3,0:T(8,128)S(1)} %get-tuple-element.20, f32[4,8,128]{2,1,0:T(8,128)S(1)} %get-tuple-element.19, pred[128,256]{0,1:T(8,128)(4,1)S(1)} %get-tuple-element.18, f32[4,8,128]{2,1,0:T(8,128)S(1)} %get-tuple-element.21, ...), kind=kLoop, calls=%fused_computation.4 | loop fusion | flops 8380416 | bytes 8519680 | tf_op jit(solution)/shard_map/reduce_sum | solution.py:42
  119.0 0.0 copy-done
  119.0 1.2 fusion.11
  120.2 1.3 %copy.29 = bf16[1,128,4096]{2,1,0:T(8,128)(2,1)} copy(bf16[1,128,4096]{1,2,0:T(8,128)(2,1)S(1)} %bitcast.87) | data formatting | bytes 2097152
  121.5 3.4 %fusion.10 = bf16[128,4,8,128]{0,3,2,1:T(8,128)(2,1)S(1)} fusion(f32[128,4,8]{0,2,1:T(8,128)S(1)} %bitcast.93, bf16[256,4,128,1]{0,2,3,1:T(8,128)(2,1)S(1)} %bitcast.91, f32[4,256,128,8]{2,1,3,0:T(8,128)} %copy-done, f32[4,8,128]{2,1,0:T(8,128)S(1)} %get-tuple-element.21, pred[128,256]{0,1:T(8,128)(4,1)S(1)} %get-tuple-element.17), kind=kOutput, calls=%fused_computation.13 | convolution fusion | flops 273678336 | bytes 5570560 | tf_op jit(solution)/shard_map/kgts,skd->tkgd/dot_general | solution.py:44
  124.9 1.3 %copy.30 = bf16[1,128,4096]{2,1,0:T(8,128)(2,1)} copy(bf16[1,128,4096]{1,2,0:T(8,128)(2,1)S(1)} %bitcast.88) | data formatting | bytes 2097152
  (4 shorter events, 0.0 us)
Async XLA Ops:
  0.6 70.6 %copy-start.1 = (s32[1,128]{1,0:T(1,128)S(1)}, s32[1,128]{1,0:T(1,128)}, u32[]{:S(2)}) copy-start(s32[1,128]{1,0:T(1,128)} %param.9) | copy-start | bytes 1540
  3.0 81.3 %copy-start.2 = (s32[1,128]{1,0:T(1,128)S(1)}, s32[1,128]{1,0:T(1,128)}, u32[]{:S(2)}) copy-start(s32[1,128]{1,0:T(1,128)} %param.11) | copy-start | bytes 1540
  3.1 26.8 %collective-permute-start = (bf16[2,64,1024]{1,2,0:T(8,128)(2,1)S(1)}, bf16[2,64,1024]{1,2,0:T(8,128)(2,1)S(1)}, u32[]{:S(2)}, u32[]{:S(2)}) collective-permute-start(bf16[2,64,1024]{1,2,0:T(8,128)(2,1)S(1)} %pad_maximum_fusion), channel_id=1, source_target_pairs={{0,48},{48,0},{96,144},{144,96},{192,240},{240,192},{288,336},{336... | collective-permute-start | bytes 786440 | tf_op jit(solution)/shard_map/ppermute | solution.py:14
  29.9 20.1 %collective-permute-start.1 = (bf16[2,64,1024]{1,2,0:T(8,128)(2,1)S(1)}, bf16[2,64,1024]{1,2,0:T(8,128)(2,1)S(1)}, u32[]{:S(2)}, u32[]{:S(2)}) collective-permute-start(bf16[2,64,1024]{1,2,0:T(8,128)(2,1)S(1)} %collective-permute-done), channel_id=1, source_target_pairs={{0,96},{48,144},{96,0},{144,48},{192,288},{240,336},{288,192},{336... | collective-permute-start | bytes 786440 | tf_op jit(solution)/shard_map/ppermute | solution.py:14
  50.0 14.8 %collective-permute-start.2 = (bf16[2,64,1024]{1,2,0:T(8,128)(2,1)S(1)}, bf16[2,64,1024]{1,2,0:T(8,128)(2,1)S(1)}, u32[]{:S(2)}, u32[]{:S(2)}) collective-permute-start(bf16[2,64,1024]{1,2,0:T(8,128)(2,1)S(1)} %collective-permute-done.1), channel_id=1, source_target_pairs={{0,192},{48,240},{96,288},{144,336},{192,0},{240,48},{288,96},{336... | collective-permute-start | bytes 786440 | tf_op jit(solution)/shard_map/ppermute | solution.py:14
  64.8 15.5 %collective-permute-start.3 = (bf16[2,64,1024]{1,2,0:T(8,128)(2,1)S(1)}, bf16[2,64,1024]{1,2,0:T(8,128)(2,1)}, u32[]{:S(2)}, u32[]{:S(2)}) collective-permute-start(bf16[2,64,1024]{1,2,0:T(8,128)(2,1)S(1)} %collective-permute-done.2), channel_id=1, source_target_pairs={{0,384},{48,432},{96,480},{144,528},{192,576},{240,624},{288,672},... | collective-permute-start | bytes 786440 | tf_op jit(solution)/shard_map/ppermute | solution.py:14
  82.4 30.7 %collective-permute-start.4 = (bf16[2,128,1024]{1,2,0:T(8,128)(2,1)}, bf16[2,128,1024]{1,2,0:T(8,128)(2,1)}, u32[]{:S(2)}, u32[]{:S(2)}) collective-permute-start(bf16[2,128,1024]{1,2,0:T(8,128)(2,1)} %pad_maximum_fusion.1), channel_id=1, source_target_pairs={{0,1},{1,2},{2,3},{3,4},{4,5},{5,6},{6,7},{7,8},{8,9},{9,10},{10,1... | collective-permute-start | bytes 1572872 | tf_op jit(solution)/shard_map/ppermute | solution.py:20
  115.5 3.5 %copy-start = (f32[4,256,128,8]{2,1,3,0:T(8,128)}, f32[4,256,128,8]{2,1,3,0:T(8,128)S(1)}, u32[]{:S(2)}) copy-start(f32[4,256,128,8]{2,1,3,0:T(8,128)S(1)} %get-tuple-element.22) | copy-start | bytes 12582916
where the time goes:
time: 127 us; the launch traced here: 126 us
  waiting for transfers between devices  85.8 us (68%)
  starting transfers between devices  17 us (13%)
  local copies, waits for them, and re-layouts  11.9 us (9%)
  matrix products  6.76 us (5%)
  other arithmetic  3.82 us (3%)
    ppermute x4, waiting for transfers between devices, swapped(): return lax.ppermute(value, axis, pairs)  58 us
    ppermute x1, waiting for transfers between devices, shifted(): lax.ppermute(value, axis, [(source, source + steps) for source in range(i...  27.8 us
    ppermute x4, starting transfers between devices, swapped(): return lax.ppermute(value, axis, pairs)  15.1 us
    unnamed x14, local copies, waits for them, and re-layouts  9.59 us
    dot_general x2, matrix products, block_attention(): jnp.einsum('kgts,skd->tkgd', weights, value_rows, preferred_element_type=...  4.59 us
  transfers between devices with their start and end apart: 5, of which 5 were waited for; matrix products, arithmetic and copies ran while one was open for 4% of the time, Pallas kernels for 0%

commit v1 on v0

v1 whole, which is shorter than its diff:
```python
import functools
import math

import jax
import jax.numpy as jnp
from jax import lax
from jax.experimental import pallas as pl
from jax.experimental.pallas import tpu as pltpu
from jax.sharding import PartitionSpec as P

KV_HEADS = 4
HEAD_DIM = 128
GROUP = 8
KV_WIDTH = KV_HEADS * HEAD_DIM
CHUNKS = 4
HEADS_DOT = 4
MESH = pl.DeviceIdType.MESH
NEG = -1e30


def mask_rows(positions, rows):
    key = lax.broadcasted_iota(jnp.int32, (2 * rows, rows), 0) - rows
    query = lax.broadcasted_iota(jnp.int32, (2 * rows, rows), 1)
    visible = (key <= query) & (key >= query - positions)
    return jnp.where(visible, 0.0, NEG).astype(jnp.bfloat16)


def attend_head(head, q_ref, kv_ref, mask_ref, eye_ref, out_ref):
    rows = q_ref.shape[0]
    factor = HEAD_DIM ** (-0.5) * math.log2(math.e)
    key_col = pl.multiple_of(head * HEAD_DIM, HEAD_DIM)
    value_col = pl.multiple_of(KV_WIDTH + head * HEAD_DIM, HEAD_DIM)
    keys = jnp.concatenate([kv_ref[:, pl.ds(key_col, HEAD_DIM)], mask_ref[...]], 1)
    values = jnp.concatenate(
        [kv_ref[:, pl.ds(value_col, HEAD_DIM)], jnp.ones((2 * rows, HEAD_DIM), jnp.bfloat16)], 1
    )
    eye = eye_ref[...]
    for first in range(0, GROUP, HEADS_DOT):
        cols = [
            pl.multiple_of(head * GROUP * HEAD_DIM + (first + g) * HEAD_DIM, HEAD_DIM)
            for g in range(HEADS_DOT)
        ]
        queries = jnp.concatenate(
            [jnp.concatenate([q_ref[:, pl.ds(c, HEAD_DIM)], eye], 1) for c in cols], 0
        )
        scores = lax.dot_general(
            queries, keys, (((1,), (1,)), ((), ())), preferred_element_type=jnp.float32
        )
        peak = jnp.max(scores, axis=1, keepdims=True)
        weights = jnp.exp2((scores - peak) * factor).astype(jnp.bfloat16)
        summed = jnp.dot(weights, values, preferred_element_type=jnp.float32)
        mixed = (summed[:, :HEAD_DIM] / summed[:, HEAD_DIM:]).astype(jnp.bfloat16)
        for g, c in enumerate(cols):
            out_ref[:, pl.ds(c, HEAD_DIM)] = mixed[g * rows : (g + 1) * rows]


def kernel(
    q_now, stash_now, pos_now, q_old, pos_old, kept, held,
    mixed_now, mixed_old, stored,
    qn, qo, on, oo, kv_now, kv_old, mask_now, mask_old, eye,
    load_sem, out_sem, send_sem, recv_sem,
):
    rows = stash_now.shape[0]
    half = kept.shape[0]
    part = half // CHUNKS
    sections = lax.axis_size("section")
    count = lax.axis_size("tp")
    s = lax.axis_index("section")
    t = lax.axis_index("tp")
    mirror = {"section": sections - 1 - s}
    right = {"tp": t + 1}
    has_right = t < count - 1
    has_left = t > 0

    loads = [
        pltpu.make_async_copy(stash_now, kv_now.at[pl.ds(rows, rows)], load_sem.at[0]),
        pltpu.make_async_copy(q_now, qn, load_sem.at[1]),
        pltpu.make_async_copy(kept, kv_old.at[pl.ds(rows, half)], load_sem.at[2]),
        pltpu.make_async_copy(q_old, qo, load_sem.at[3]),
    ]
    for load in loads:
        load.start()

    barrier = pltpu.get_barrier_semaphore()
    pl.semaphore_signal(barrier, inc=1, device_id=mirror, device_id_type=MESH)

    @pl.when(has_right)
    def _():
        pl.semaphore_signal(barrier, inc=1, device_id=right, device_id_type=MESH)

    @pl.when(has_left)
    def _():
        pl.semaphore_signal(barrier, inc=1, device_id={"tp": t - 1}, device_id_type=MESH)

    pl.semaphore_wait(
        barrier, 1 + has_right.astype(jnp.int32) + has_left.astype(jnp.int32)
    )

    def remote(index, src, dst, device):
        return pltpu.make_async_remote_copy(
            src_ref=src, dst_ref=dst, send_sem=send_sem.at[index], recv_sem=recv_sem.at[index],
            device_id=device, device_id_type=MESH,
        )

    swap = [
        remote(
            c, held.at[pl.ds(c * part, part)],
            kv_old.at[pl.ds(rows + half + c * part, part)], mirror,
        )
        for c in range(CHUNKS)
    ]
    pass_on = [
        remote(
            CHUNKS + c, kv_old.at[pl.ds(rows + half + c * part, part)],
            kv_old.at[pl.ds(half + c * part, part)], right,
        )
        for c in range(CHUNKS)
    ]
    shift_now = remote(2 * CHUNKS, stash_now, kv_now.at[pl.ds(0, rows)], right)
    shift_kept = remote(2 * CHUNKS + 1, kept, kv_old.at[pl.ds(0, half)], right)
    evict = remote(2 * CHUNKS + 2, stash_now.at[pl.ds(rows - half, half)], stored, mirror)

    for copy in swap:
        copy.start()

    @pl.when(has_right)
    def _():
        shift_now.start()
        shift_kept.start()

    evict.start()

    @pl.when(jnp.logical_not(has_left))
    def _():
        kv_now[pl.ds(0, rows), :] = jnp.zeros((rows, 2 * KV_WIDTH), jnp.bfloat16)
        kv_old[pl.ds(0, rows), :] = jnp.zeros((rows, 2 * KV_WIDTH), jnp.bfloat16)

    eye[...] = jnp.where(
        lax.broadcasted_iota(jnp.int32, (rows, rows), 0)
        == lax.broadcasted_iota(jnp.int32, (rows, rows), 1),
        1.0, 0.0,
    ).astype(jnp.bfloat16)
    mask_now[...] = mask_rows(pos_now[...], rows)
    mask_old[...] = mask_rows(pos_old[...], rows)

    loads[0].wait()
    loads[1].wait()

    @pl.when(has_left)
    def _():
        shift_now.wait_recv()

    width = GROUP * HEAD_DIM

    def flush(out_v, out_h, head, index):
        col = pl.multiple_of(head * width, width)
        return pltpu.make_async_copy(
            out_v.at[:, pl.ds(col, width)], out_h.at[:, pl.ds(col, width)], out_sem.at[index]
        )

    for head in range(KV_HEADS):
        attend_head(head, qn, kv_now, mask_now, eye, on)
        flush(on, mixed_now, head, head).start()
        for c in range(head * CHUNKS // KV_HEADS, (head + 1) * CHUNKS // KV_HEADS):
            swap[c].wait_recv()

            @pl.when(has_right)
            def _(c=c):
                pass_on[c].start()

    loads[2].wait()
    loads[3].wait()

    @pl.when(has_left)
    def _():
        shift_kept.wait_recv()
        for copy in pass_on:
            copy.wait_recv()

    for head in range(KV_HEADS):
        attend_head(head, qo, kv_old, mask_old, eye, oo)
        flush(oo, mixed_old, head, KV_HEADS + head).start()

    for head in range(KV_HEADS):
        flush(on, mixed_now, head, head).wait()
        flush(oo, mixed_old, head, KV_HEADS + head).wait()

    for copy in swap:
        copy.wait_send()

    @pl.when(has_right)
    def _():
        shift_now.wait_send()
        shift_kept.wait_send()
        for copy in pass_on:
            copy.wait_send()

    evict.wait()


def body(queries_now, stash_now, positions_now, queries_old, positions_old, stash_kept, stash_held):
    rows, width = queries_now.shape[1:]
    half, kv_width = stash_kept.shape[1:]
    bf16 = jnp.bfloat16
    hbm = pl.BlockSpec(memory_space=pl.ANY)
    vmem = pl.BlockSpec(memory_space=pltpu.VMEM)
    remote_count = 2 * CHUNKS + 3
    mixed_now, mixed_old, stored = pl.pallas_call(
        kernel,
        out_shape=(
            jax.ShapeDtypeStruct((rows, width), bf16),
            jax.ShapeDtypeStruct((rows, width), bf16),
            jax.ShapeDtypeStruct((half, kv_width), bf16),
        ),
        in_specs=[hbm, hbm, vmem, hbm, vmem, hbm, hbm],
        out_specs=(hbm, hbm, hbm),
        scratch_shapes=[
            pltpu.VMEM((rows, width), bf16),
            pltpu.VMEM((rows, width), bf16),
            pltpu.VMEM((rows, width), bf16),
            pltpu.VMEM((rows, width), bf16),
            pltpu.VMEM((2 * rows, kv_width), bf16),
            pltpu.VMEM((2 * rows, kv_width), bf16),
            pltpu.VMEM((2 * rows, rows), bf16),
            pltpu.VMEM((2 * rows, rows), bf16),
            pltpu.VMEM((rows, rows), bf16),
            pltpu.SemaphoreType.DMA((4,)),
            pltpu.SemaphoreType.DMA((2 * KV_HEADS,)),
            pltpu.SemaphoreType.DMA((remote_count,)),
            pltpu.SemaphoreType.DMA((remote_count,)),
        ],
        compiler_params=pltpu.CompilerParams(collective_id=0, has_side_effects=True),
        name="relay_attention",
    )(
        queries_now[0], stash_now[0], positions_now, queries_old[0], positions_old,
        stash_kept[0], stash_held[0],
    )
    return (mixed_now[None], mixed_old[None], stored[None])


def solution(mesh):
    return jax.shard_map(
        body,
        mesh=mesh,
        in_specs=(
            P("section", "tp", None),
            P("section", "tp", None),
            P("section", "tp"),
            P("section", "tp", None),
            P("section", "tp"),
            P("section", "tp", None),
            P("section", "tp", None),
        ),
        out_specs=(P("section", "tp", None), P("section", "tp", None), P("section", "tp", None)),
        check_vma=False,
    )
```

time: 127 us -> 38.7 us (0.30)
  the two profiles are of different devices: /device:TPU:12 before, /device:TPU:62 now
where the time goes in v1:
time: 38.7 us; the launch traced here: 38.5 us
  Pallas kernels  33.8 us (87%)
  local copies, waits for them, and re-layouts  4.06 us (10%)
  between operations  0.65 us (2%)
    pallas_call x1, Pallas kernels, body(): pl.pallas_call(kernel, out_shape=(jax.ShapeDtypeStruct((rows, width), bf1...  33.8 us
    unnamed x7, local copies, waits for them, and re-layouts  4.06 us

profile of v1, /device:TPU:62, one launch (start us, length us, event | category | flops | bytes accessed | tf_op | source)
XLA Modules:
  0.0 38.5 jit_solution(1054210156740041358)
XLA Ops:
  0.6 33.8 %relay_attention.1 = (bf16[128,4096]{1,0:T(8,128)(2,1)}, bf16[128,4096]{1,0:T(8,128)(2,1)}, bf16[64,1024]{1,0:T(8,128)(2,1)}) custom-call(bf16[128,4096]{1,0:T(8,128)(2,1)} %bitcast.8, bf16[128,1024]{1,0:T(8,128)(2,1)} %bitcast.12, s32[1,128]{1,0:T(1,128)} %pos_now.1, bf16[128,4096]{1,0:T(8,128)(2,1)} %bitcast.9, s32[1,128]{1,0:T(1,128)} %pos_old.1, ...), custom_call_target="tpu_custom_call" | custom-call | tf_op jit(solution)/shard_map/relay_attention/pallas_call | solution.py:208
  34.4 0.0 copy-start
  34.4 2.4 %copy.13 = bf16[1,128,4096]{2,1,0:T(8,128)(2,1)} copy(bf16[1,128,4096]{2,1,0:T(8,128)(2,1)} %bitcast.11) | data formatting | bytes 2097152
  36.8 0.0 copy-done
  36.8 0.0 copy-start.1
  36.8 1.0 %copy.14 = bf16[1,128,4096]{2,1,0:T(8,128)(2,1)} copy(bf16[1,128,4096]{2,1,0:T(8,128)(2,1)S(1)} %bitcast.10) | data formatting | bytes 2097152
  37.8 0.1 copy-done.1
  37.8 0.7 %copy.15 = bf16[1,64,1024]{2,1,0:T(8,128)(2,1)} copy(bf16[1,64,1024]{2,1,0:T(8,128)(2,1)S(1)} %bitcast.15) | data formatting | bytes 262144
Async XLA Ops:
  34.4 2.4 %copy-start = (bf16[128,4096]{1,0:T(8,128)(2,1)S(1)}, bf16[128,4096]{1,0:T(8,128)(2,1)}, u32[]{:S(2)}) copy-start(bf16[128,4096]{1,0:T(8,128)(2,1)} %get-tuple-element.7) | copy-start | bytes 3145732
  36.8 1.0 %copy-start.1 = (bf16[64,1024]{1,0:T(8,128)(2,1)S(1)}, bf16[64,1024]{1,0:T(8,128)(2,1)}, u32[]{:S(2)}) copy-start(bf16[64,1024]{1,0:T(8,128)(2,1)} %get-tuple-element.8) | copy-start | bytes 393220

commit v2 on v1

--- a/solution.py
+++ b/solution.py
@@ -57,8 +57,8 @@
 def kernel(
     q_now, stash_now, pos_now, q_old, pos_old, kept, held,
     mixed_now, mixed_old, stored,
-    qn, qo, on, oo, kv_now, kv_old, mask_now, mask_old, eye,
-    load_sem, out_sem, send_sem, recv_sem,
+    qn, qo, kv_now, kv_old, mask_now, mask_old, eye,
+    load_sem, send_sem, recv_sem,
 ):
     rows = stash_now.shape[0]
     half = kept.shape[0]
@@ -71,6 +71,12 @@
     right = {"tp": t + 1}
     has_right = t < count - 1
     has_left = t > 0
+    seam = count // 2
+    gives_direct = t == seam - 1
+    takes_direct = t == seam
+    forwards_first = (t == 0) | (t == seam)
+    passes_on = has_right & jnp.logical_not(gives_direct)
+    takes_passed = has_left & jnp.logical_not(takes_direct)
 
     loads = [
         pltpu.make_async_copy(stash_now, kv_now.at[pl.ds(rows, rows)], load_sem.at[0]),
@@ -84,16 +90,18 @@
     barrier = pltpu.get_barrier_semaphore()
     pl.semaphore_signal(barrier, inc=1, device_id=mirror, device_id_type=MESH)
 
-    @pl.when(has_right)
-    def _():
-        pl.semaphore_signal(barrier, inc=1, device_id=right, device_id_type=MESH)
-
     @pl.when(has_left)
     def _():
         pl.semaphore_signal(barrier, inc=1, device_id={"tp": t - 1}, device_id_type=MESH)
 
+    @pl.when(takes_direct)
+    def _():
+        pl.semaphore_signal(
+            barrier, inc=1, device_id={"section": sections - 1 - s, "tp": t - 1}, device_id_type=MESH
+        )
+
     pl.semaphore_wait(
-        barrier, 1 + has_right.astype(jnp.int32) + has_left.astype(jnp.int32)
+        barrier, 1 + has_right.astype(jnp.int32) + gives_direct.astype(jnp.int32)
     )
 
     def remote(index, src, dst, device):
@@ -118,6 +126,10 @@
     ]
     shift_now = remote(2 * CHUNKS, stash_now, kv_now.at[pl.ds(0, rows)], right)
     shift_kept = remote(2 * CHUNKS + 1, kept, kv_old.at[pl.ds(0, half)], right)
+    direct = remote(
+        2 * CHUNKS + 3, held, kv_old.at[pl.ds(half, half)],
+        {"section": sections - 1 - s, "tp": t + 1},
+    )
     evict = remote(2 * CHUNKS + 2, stash_now.at[pl.ds(rows - half, half)], stored, mirror)
 
     for copy in swap:
@@ -127,6 +139,10 @@
     def _():
         shift_now.start()
         shift_kept.start()
+
+    @pl.when(gives_direct)
+    def _():
+        direct.start()
 
     evict.start()
 
@@ -143,6 +159,12 @@
     mask_now[...] = mask_rows(pos_now[...], rows)
     mask_old[...] = mask_rows(pos_old[...], rows)
 
+    @pl.when(forwards_first)
+    def _():
+        for c in range(CHUNKS):
+            swap[c].wait_recv()
+            pass_on[c].start()
+
     loads[0].wait()
     loads[1].wait()
 
@@ -150,21 +172,15 @@
     def _():
         shift_now.wait_recv()
 
-    width = GROUP * HEAD_DIM
-
-    def flush(out_v, out_h, head, index):
-        col = pl.multiple_of(head * width, width)
-        return pltpu.make_async_copy(
-            out_v.at[:, pl.ds(col, width)], out_h.at[:, pl.ds(col, width)], out_sem.at[index]
-        )
-
     for head in range(KV_HEADS):
-        attend_head(head, qn, kv_now, mask_now, eye, on)
-        flush(on, mixed_now, head, head).start()
+        attend_head(head, qn, kv_now, mask_now, eye, mixed_now)
         for c in range(head * CHUNKS // KV_HEADS, (head + 1) * CHUNKS // KV_HEADS):
-            swap[c].wait_recv()
-
-            @pl.when(has_right)
+
+            @pl.when(jnp.logical_not(forwards_first))
+            def _(c=c):
+                swap[c].wait_recv()
+
+            @pl.when(passes_on & jnp.logical_not(forwards_first))
             def _(c=c):
                 pass_on[c].start()
 
@@ -174,16 +190,18 @@
     @pl.when(has_left)
     def _():
         shift_kept.wait_recv()
+
+    @pl.when(takes_passed)
+    def _():
         for copy in pass_on:
             copy.wait_recv()
 
+    @pl.when(takes_direct)
+    def _():
+        direct.wait_recv()
+
     for head in range(KV_HEADS):
-        attend_head(head, qo, kv_old, mask_old, eye, oo)
-        flush(oo, mixed_old, head, KV_HEADS + head).start()
-
-    for head in range(KV_HEADS):
-        flush(on, mixed_now, head, head).wait()
-        flush(oo, mixed_old, head, KV_HEADS + head).wait()
+        attend_head(head, qo, kv_old, mask_old, eye, mixed_old)
 
     for copy in swap:
         copy.wait_send()
@@ -192,10 +210,29 @@
     def _():
         shift_now.wait_send()
         shift_kept.wait_send()
+
+    @pl.when(passes_on)
+    def _():
         for copy in pass_on:
             copy.wait_send()
 
+    @pl.when(gives_direct)
+    def _():
+        direct.wait_send()
+
     evict.wait()
+
+
+def write_out(now_in, old_in, stored_in, now_out, old_out, stored_out, sem):
+    copies = [
+        pltpu.make_async_copy(now_in, now_out, sem.at[0]),
+        pltpu.make_async_copy(old_in, old_out, sem.at[1]),
+        pltpu.make_async_copy(stored_in, stored_out, sem.at[2]),
+    ]
+    for copy in copies:
+        copy.start()
+    for copy in copies:
+        copy.wait()
 
 
 def body(queries_now, stash_now, positions_now, queries_old, positions_old, stash_kept, stash_held):
@@ -204,19 +241,17 @@
     bf16 = jnp.bfloat16
     hbm = pl.BlockSpec(memory_space=pl.ANY)
     vmem = pl.BlockSpec(memory_space=pltpu.VMEM)
-    remote_count = 2 * CHUNKS + 3
+    remote_count = 2 * CHUNKS + 4
     mixed_now, mixed_old, stored = pl.pallas_call(
         kernel,
         out_shape=(
-            jax.ShapeDtypeStruct((rows, width), bf16),
-            jax.ShapeDtypeStruct((rows, width), bf16),
-            jax.ShapeDtypeStruct((half, kv_width), bf16),
+            pltpu.VMEM((rows, width), bf16),
+            pltpu.VMEM((rows, width), bf16),
+            pltpu.VMEM((half, kv_width), bf16),
         ),
         in_specs=[hbm, hbm, vmem, hbm, vmem, hbm, hbm],
-        out_specs=(hbm, hbm, hbm),
+        out_specs=(vmem, vmem, vmem),
         scratch_shapes=[
-            pltpu.VMEM((rows, width), bf16),
-            pltpu.VMEM((rows, width), bf16),
             pltpu.VMEM((rows, width), bf16),
             pltpu.VMEM((rows, width), bf16),
             pltpu.VMEM((2 * rows, kv_width), bf16),
@@ -225,7 +260,6 @@
             pltpu.VMEM((2 * rows, rows), bf16),
             pltpu.VMEM((rows, rows), bf16),
             pltpu.SemaphoreType.DMA((4,)),
-            pltpu.SemaphoreType.DMA((2 * KV_HEADS,)),
             pltpu.SemaphoreType.DMA((remote_count,)),
             pltpu.SemaphoreType.DMA((remote_count,)),
         ],
@@ -235,6 +269,16 @@
         queries_now[0], stash_now[0], positions_now, queries_old[0], positions_old,
         stash_kept[0], stash_held[0],
     )
+    shapes = tuple(jax.ShapeDtypeStruct(a.shape, a.dtype) for a in (mixed_now, mixed_old, stored))
+    mixed_now, mixed_old, stored = pl.pallas_call(
+        write_out,
+        out_shape=shapes,
+        in_specs=[pl.BlockSpec(memory_space=pl.ANY)] * 3,
+        out_specs=(hbm, hbm, hbm),
+        scratch_shapes=[pltpu.SemaphoreType.DMA((3,))],
+        compiler_params=pltpu.CompilerParams(vmem_limit_bytes=2**20),
+        name="write_out",
+    )(mixed_now, mixed_old, stored)
     return (mixed_now[None], mixed_old[None], stored[None])
 
 

time: 38.7 us -> 30.7 us (0.79)
  the two profiles are of different devices: /device:TPU:62 before, /device:TPU:46 now
where the time goes in v2:
time: 30.7 us; the launch traced here: 30.5 us
  Pallas kernels  29.9 us (97%)
  between operations  0.64 us (2%)
    pallas_call x1, Pallas kernels, body(): pl.pallas_call(kernel, out_shape=(pltpu.VMEM((rows, width), bf16), pltpu....  28.5 us
    pallas_call x1, Pallas kernels, body(): pl.pallas_call(write_out, out_shape=shapes, in_specs=[pl.BlockSpec(memory...  1.37 us

profile of v2, /device:TPU:46, one launch (start us, length us, event | category | flops | bytes accessed | tf_op | source)
XLA Modules:
  0.0 30.5 jit_solution(2194248777714036554)
XLA Ops:
  0.6 28.5 %relay_attention.1 = (bf16[128,4096]{1,0:T(8,128)(2,1)S(1)}, bf16[128,4096]{1,0:T(8,128)(2,1)S(1)}, bf16[64,1024]{1,0:T(8,128)(2,1)S(1)}) custom-call(bf16[128,4096]{1,0:T(8,128)(2,1)} %bitcast.8, bf16[128,1024]{1,0:T(8,128)(2,1)} %bitcast.10, s32[1,128]{1,0:T(1,128)} %pos_now.1, bf16[128,4096]{1,0:T(8,128)(2,1)} %bitcast.9, s32[1,128]{1,0:T(1,128)} %pos_old.1, ...), custom_call_target="tpu_custom_call" | custom-call | tf_op jit(solution)/shard_map/relay_attention/pallas_call | solution.py:245
  29.2 1.4 %write_out.1 = (bf16[128,4096]{1,0:T(8,128)(2,1)}, bf16[128,4096]{1,0:T(8,128)(2,1)}, bf16[64,1024]{1,0:T(8,128)(2,1)}) custom-call(bf16[128,4096]{1,0:T(8,128)(2,1)S(1)} %get-tuple-element.9.now_in, bf16[128,4096]{1,0:T(8,128)(2,1)S(1)} %get-tuple-element.10.old_in, bf16[64,1024]{1,0:T(8,128)(2,1)S(1)} %get-tuple-element.11.stored_in), custom_call_target="tpu_custom_call" | custom-call | tf_op jit(solution)/shard_map/write_out/pallas_call | solution.py:273

commit v3 on v2

--- a/solution.py
+++ b/solution.py
@@ -58,7 +58,7 @@
     q_now, stash_now, pos_now, q_old, pos_old, kept, held,
     mixed_now, mixed_old, stored,
     qn, qo, kv_now, kv_old, mask_now, mask_old, eye,
-    load_sem, send_sem, recv_sem,
+    load_sem, send_sem, recv_sem, go_sem,
 ):
     rows = stash_now.shape[0]
     half = kept.shape[0]
@@ -74,6 +74,7 @@
     seam = count // 2
     gives_direct = t == seam - 1
     takes_direct = t == seam
+    tells = t == seam - 2
     forwards_first = (t == 0) | (t == seam)
     passes_on = has_right & jnp.logical_not(gives_direct)
     takes_passed = has_left & jnp.logical_not(takes_direct)
@@ -88,7 +89,11 @@
         load.start()
 
     barrier = pltpu.get_barrier_semaphore()
-    pl.semaphore_signal(barrier, inc=1, device_id=mirror, device_id_type=MESH)
+    pl.semaphore_signal(
+        barrier, inc=1,
+        device_id={"section": sections - 1 - s, "tp": t - gives_direct.astype(jnp.int32)},
+        device_id_type=MESH,
+    )
 
     @pl.when(has_left)
     def _():
@@ -101,8 +106,12 @@
         )
 
     pl.semaphore_wait(
-        barrier, 1 + has_right.astype(jnp.int32) + gives_direct.astype(jnp.int32)
-    )
+        barrier, 1 + has_right.astype(jnp.int32) + tells.astype(jnp.int32)
+    )
+
+    @pl.when(tells)
+    def _():
+        pl.semaphore_signal(go_sem, inc=1, device_id=right, device_id_type=MESH)
 
     def remote(index, src, dst, device):
         return pltpu.make_async_remote_copy(
@@ -132,8 +141,14 @@
     )
     evict = remote(2 * CHUNKS + 2, stash_now.at[pl.ds(rows - half, half)], stored, mirror)
 
-    for copy in swap:
-        copy.start()
+    @pl.when(jnp.logical_not(gives_direct))
+    def _():
+        for copy in swap:
+            copy.start()
+
+    @pl.when(gives_direct)
+    def _():
+        direct.start()
 
     @pl.when(has_right)
     def _():
@@ -142,7 +157,9 @@
 
     @pl.when(gives_direct)
     def _():
-        direct.start()
+        pl.semaphore_wait(go_sem, 1)
+        for copy in swap:
+            copy.start()
 
     evict.start()
 
@@ -262,6 +279,7 @@
             pltpu.SemaphoreType.DMA((4,)),
             pltpu.SemaphoreType.DMA((remote_count,)),
             pltpu.SemaphoreType.DMA((remote_count,)),
+            pltpu.SemaphoreType.REGULAR,
         ],
         compiler_params=pltpu.CompilerParams(collective_id=0, has_side_effects=True),
         name="relay_attention",

time: 30.7 us -> 29.6 us (0.964)
  the two profiles are of different devices: /device:TPU:46 before, /device:TPU:40 now
where the time goes in v3:
time: 29.6 us; the launch traced here: 29.4 us
  Pallas kernels  28.8 us (97%)
  between operations  0.64 us (2%)
    pallas_call x1, Pallas kernels, body(): pl.pallas_call(kernel, out_shape=(pltpu.VMEM((rows, width), bf16), pltpu....  27.4 us
    pallas_call x1, Pallas kernels, body(): pl.pallas_call(write_out, out_shape=shapes, in_specs=[pl.BlockSpec(memory...  1.37 us

profile of v3, /device:TPU:40, one launch (start us, length us, event | category | flops | bytes accessed | tf_op | source)
XLA Modules:
  0.0 29.4 jit_solution(8408801405190912231)
XLA Ops:
  0.6 27.4 %relay_attention.1 = (bf16[128,4096]{1,0:T(8,128)(2,1)S(1)}, bf16[128,4096]{1,0:T(8,128)(2,1)S(1)}, bf16[64,1024]{1,0:T(8,128)(2,1)S(1)}) custom-call(bf16[128,4096]{1,0:T(8,128)(2,1)} %bitcast.8, bf16[128,1024]{1,0:T(8,128)(2,1)} %bitcast.10, s32[1,128]{1,0:T(1,128)} %pos_now.1, bf16[128,4096]{1,0:T(8,128)(2,1)} %bitcast.9, s32[1,128]{1,0:T(1,128)} %pos_old.1, ...), custom_call_target="tpu_custom_call" | custom-call | tf_op jit(solution)/shard_map/relay_attention/pallas_call | solution.py:262
  28.1 1.4 %write_out.1 = (bf16[128,4096]{1,0:T(8,128)(2,1)}, bf16[128,4096]{1,0:T(8,128)(2,1)}, bf16[64,1024]{1,0:T(8,128)(2,1)}) custom-call(bf16[128,4096]{1,0:T(8,128)(2,1)S(1)} %get-tuple-element.9.now_in, bf16[128,4096]{1,0:T(8,128)(2,1)S(1)} %get-tuple-element.10.old_in, bf16[64,1024]{1,0:T(8,128)(2,1)S(1)} %get-tuple-element.11.stored_in), custom_call_target="tpu_custom_call" | custom-call | tf_op jit(solution)/shard_map/write_out/pallas_call | solution.py:291
